TPU v7x, 32 devices: a whole 2x2x4 slice. The times are simulated.
32 devices in a mesh: rep: 2 (over x), node: 2 (over core), local: 8 (over z, y).
Axes of the slice: x: 2, y: 2, z: 4, core: 2. Of those that a mesh axis runs over, the one named last changes fastest.
Arguments:
- attn_out: bfloat16 [64, 1024], P(('rep', 'node'), 'local'), parts along dimension 0, may hold values from -6 to 6
- o_proj: bfloat16 [1024, 7168], P('local'), may hold values from -0.1875 to 0.1875
- resid: bfloat16 [64, 7168], P(('rep', 'node', 'local')), parts along dimension 0, may hold values from -6 to 6
- norm_gain: float32 [7168], replicated, may hold values from 0.5 to 1.5
- routes: int32 [64, 8], P(('rep', 'node', 'local')), parts along dimension 0, may hold values from 0 to 15, all different within a row; in each aligned block of 2 rows (0 to 1, 2 to 3, ...) at most 2 rows name the same one
- route_w: bfloat16 [64, 8], P(('rep', 'node', 'local')), parts along dimension 0, may hold values from 0.19921875 to 1
- w_gate: bfloat16 [16, 7168, 2048], P(('node', 'local')), may hold values from -0.0625 to 0.0625
- w_up: bfloat16 [16, 7168, 2048], P(('node', 'local')), may hold values from -0.0625 to 0.0625
- w_down: bfloat16 [16, 2048, 7168], P(('node', 'local')), may hold values from -0.125 to 0.125
Outputs:
- layer_out: bfloat16 [64, 7168], P(('rep', 'node', 'local')), parts along dimension 0
There are 2 independent parts, one for each index of `rep`. A program takes and returns all parts, laid end to end along the dimension named above; an argument that names none is the same for every part. Nothing has to cross between parts.
Inputs may be any that keep to these rules, and one draw needn't show every extreme that they name: `routes`: each row names 8 different experts. Within the rows of one device (aligned blocks of 2 rows) no expert is named more than 2 times, and in some block some expert is named exactly 2 times.
All inputs are finite; a program needn't handle non-finite values.
Results may differ from a plain program's by a relative error of at most 0.0075.
Values may be sent and summed in bfloat16 or wider, within the bound.
A program may use at most 128 MiB of HBM per device.

v0:
```python
import jax
import jax.numpy as jnp
from jax import lax
from jax.sharding import PartitionSpec as P

GROUP_EXPERTS = 8
MOST = 2


def plan_slots(expert_ids, pair_weights, expert_count, capacity, token_count):
    pair_count = expert_ids.shape[0]
    pairs_per_token = pair_count // token_count
    expert_hot = (expert_ids[:, None] == jnp.arange(expert_count, dtype=jnp.int32)[None, :]).astype(
        jnp.int32
    )
    earlier = jnp.cumsum(expert_hot, axis=0) - expert_hot
    slot_ids = jnp.sum(earlier * expert_hot, axis=1)
    usable = jnp.sum(expert_hot, axis=1) > 0
    position = expert_ids * capacity + slot_ids
    placed = (
        (position[:, None] == jnp.arange(expert_count * capacity, dtype=jnp.int32)[None, :])
        & usable[:, None]
    ).astype(jnp.float32)
    pair_token = jnp.arange(pair_count, dtype=jnp.int32) // pairs_per_token
    token_hot = (pair_token[:, None] == jnp.arange(token_count, dtype=jnp.int32)[None, :]).astype(
        jnp.float32
    )
    select = jnp.dot(
        placed.T, token_hot, precision=lax.Precision.HIGHEST, preferred_element_type=jnp.float32
    )
    combine = jnp.dot(
        token_hot.T,
        placed * pair_weights[:, None],
        precision=lax.Precision.HIGHEST,
        preferred_element_type=jnp.float32,
    )
    return (select, combine)


def run_expert(received, w_gate, w_up, w_down):
    senders, slot_count, model_width = received.shape
    flat_rows = received.reshape(senders * slot_count, model_width)
    gate_val = jnp.dot(flat_rows, w_gate[0], preferred_element_type=jnp.float32)
    up_val = jnp.dot(flat_rows, w_up[0], preferred_element_type=jnp.float32)
    activated = (jax.nn.silu(gate_val) * up_val).astype(jnp.bfloat16)
    pieces = jnp.dot(activated, w_down[0], preferred_element_type=jnp.float32).astype(jnp.bfloat16)
    return pieces.reshape(senders, slot_count, model_width)


def shards(attn_out, o_proj, resid, norm_gain, routes, route_w, w_gate, w_up, w_down):
    tok_rows = resid.shape[0]
    model_width = resid.shape[1]
    projected = lax.psum_scatter(
        jnp.dot(attn_out, o_proj, preferred_element_type=jnp.float32),
        "local",
        scatter_dimension=0,
        tiled=True,
    )
    hidden = resid.astype(jnp.float32) + projected
    mean_sq = jnp.mean(hidden * hidden, axis=-1, keepdims=True)
    normed = (hidden * lax.rsqrt(mean_sq + 1e-06) * norm_gain).astype(jnp.bfloat16)
    node_count = lax.axis_size("node")
    shard_count = lax.axis_size("local") // GROUP_EXPERTS
    summed = hidden
    expert_count = node_count * GROUP_EXPERTS
    select, combine = plan_slots(
        routes.reshape(-1), route_w.reshape(-1).astype(jnp.float32), expert_count, MOST, tok_rows
    )
    slot_rows = jnp.dot(
        select.astype(jnp.bfloat16), normed, preferred_element_type=jnp.float32
    ).astype(jnp.bfloat16)
    shaped = slot_rows.reshape(expert_count, 1, MOST, model_width)
    widened = jnp.broadcast_to(shaped, (expert_count, shard_count, MOST, model_width))
    returned = lax.all_to_all(
        run_expert(
            lax.all_to_all(
                widened.reshape(expert_count * shard_count, MOST, model_width),
                ("node", "local"),
                split_axis=0,
                concat_axis=0,
                tiled=True,
            ),
            w_gate,
            w_up,
            w_down,
        ),
        ("node", "local"),
        split_axis=0,
        concat_axis=0,
        tiled=True,
    )
    shaped = returned.reshape(expert_count, shard_count, MOST, model_width).astype(jnp.float32)
    expert_out = jnp.sum(shaped, axis=1).reshape(expert_count * MOST, model_width)
    slot_group = jnp.arange(expert_count * MOST, dtype=jnp.int32) // (MOST * GROUP_EXPERTS)
    for group_idx in range(node_count):
        masked = combine * (slot_group == group_idx).astype(jnp.float32)[None, :]
        group_out = jnp.dot(
            masked, expert_out, precision=lax.Precision.HIGHEST, preferred_element_type=jnp.float32
        ).astype(jnp.bfloat16)
        summed = summed + group_out.astype(jnp.float32)
    return summed.astype(jnp.bfloat16)


def solution(mesh):
    placed = (
        P(("rep", "node"), "local"),
        P("local", None),
        P(("rep", "node", "local"), None),
        P(),
        P(("rep", "node", "local"), None),
        P(("rep", "node", "local"), None),
        P(("node", "local"), None, None),
        P(("node", "local"), None, None),
        P(("node", "local"), None, None),
    )
    return jax.shard_map(
        shards,
        mesh=mesh,
        in_specs=placed,
        out_specs=P(("rep", "node", "local"), None),
        check_vma=False,
    )
```

profile of v0, /device:TPU:0, one launch (start us, length us, event | category | flops | bytes accessed | tf_op | source)
XLA Modules:
  0.0 167.8 jit_solution(16744512488504878344)
XLA Ops:
  6.5 1.5 copy-done
  8.0 1.8 %fusion.50 = f32[16,7168]{1,0:T(8,128)} fusion(bf16[16,128]{1,0:T(8,128)(2,1)} %param.9, bf16[128,7168]{1,0:T(8,128)(2,1)S(1)} %copy-done), kind=kOutput, calls=%fused_computation.64 | convolution fusion | flops 29360128 | bytes 2297856 | tf_op jit(solution)/shard_map/dot_general | solution.py:54
  9.9 0.0 all-reduce.3.cloned.1.call-update
  9.9 0.8 reshape.78
  10.6 0.1 fusion.31
  10.8 0.2 fusion.35
  11.0 1.2 dynamic-slice
  12.9 0.3 convolution_convert_fusion.3
  13.1 72.8 %all-reduce.3.cloned.1.call-done = f32[16,7168]{1,0:T(8,128)} async-done(((f32[16,7168]{1,0:T(8,128)}), f32[16,7168]{1,0:T(8,128)}) %all-reduce.3.cloned.1.call-update) | async-done | bytes 458768
  85.9 1.1 multiply_reduce_fusion
  87.0 1.3 convolution_convert_fusion
  88.3 0.2 reshape_reshape.3
  88.5 18.2 %all_to_all.10 = bf16[16,2,7168]{2,1,0:T(2,128)(2,1)S(1)} all-to-all(bf16[16,2,7168]{2,1,0:T(2,128)(2,1)S(1)} %reshape_reshape.3), channel_id=1, replica_groups=mesh['rep'=2,'node'=2,'local'=8] {'node','local'}, dimensions={0} | all-to-all | bytes 917504 | tf_op jit(solution)/shard_map/all_to_all | solution.py:76
  106.7 0.2 reshape.79
  106.9 12.0 %fusion.4 = f32[32,2048]{1,0:T(8,128)S(1)} fusion(bf16[32,7168]{1,0:T(8,128)(2,1)S(1)} %reshape.79, bf16[1,7168,2048]{2,1,0:T(8,128)(2,1)} %param.15), kind=kOutput, calls=%fused_computation.4 | convolution fusion | flops 939524096 | bytes 30081024 | tf_op jit(solution)/shard_map/dot_general | solution.py:43
  118.9 20.8 %fusion.6 = bf16[32,7168]{1,0:T(8,128)(2,1)S(1)} fusion(bf16[1,2048,7168]{2,1,0:T(8,128)(2,1)} %param.17, bf16[32,7168]{1,0:T(8,128)(2,1)S(1)} %reshape.79, bf16[1,7168,2048]{2,1,0:T(8,128)(2,1)} %param.16, f32[32,2048]{1,0:T(8,128)S(1)} %fusion.4), kind=kOutput, calls=%fused_computation.6 | convolution fusion | flops 1879670784 | bytes 59899904 | tf_op jit(solution)/shard_map/dot_general | solution.py:46
  139.7 1.0 reshape.80
  140.6 3.6 %all-to-all-start.1 = ((bf16[16,2,7168]{2,1,0:T(2,128)(2,1)}), bf16[16,2,7168]{2,1,0:T(2,128)(2,1)S(1)}, u32[]{:S(2)}, u32[]{:S(2)}) async-start(bf16[16,2,7168]{2,1,0:T(2,128)(2,1)} %reshape.80), calls=%async_computation.1 | async-start | bytes 917504 | tf_op jit(solution)/shard_map/all_to_all | solution.py:74
  144.2 0.1 reshape.82
  144.3 0.3 fusion.29
  144.6 14.0 %all-to-all-done.1 = bf16[16,2,7168]{2,1,0:T(2,128)(2,1)S(1)} async-done(((bf16[16,2,7168]{2,1,0:T(2,128)(2,1)}), bf16[16,2,7168]{2,1,0:T(2,128)(2,1)S(1)}, u32[]{:S(2)}, u32[]{:S(2)}) %all-to-all-start.1) | async-done | bytes 458784 | tf_op jit(solution)/shard_map/all_to_all | solution.py:74
  158.6 0.2 reshape.81
  158.8 0.3 fusion.13
  159.1 1.9 %fusion.12 = bf16[2,7168]{1,0:T(2,128)(2,1)} fusion(f32[2,7168]{1,0:T(2,128)S(1)} %fusion.13, bf16[32,7168]{1,0:T(8,128)(2,1)S(1)} %reshape.81, f32[2,32]{1,0:T(2,128)S(1)} %fusion.29, f32[32]{0:T(128)S(1)} %compare_convert_fusion.1, f32[16,7168]{1,0:T(8,128)} %all-reduce.3.cloned.1.call-done, u32[]{:T(128)S(6)} %multiply.7, bf16[2,7168]{1,0:T(2,128)(2,1)S(1)} %copy-done.1), kind=kOutput, calls=%fused_computation.13 | convolution fusion | flops 5605440 | bytes 631172 | tf_op jit(solution)/shard_map/dot_general | solution.py:97
  (12 shorter events, 0.1 us)
Async XLA Ops:
  6.5 1.5 copy-start
  6.5 79.3 %all-reduce.3.cloned.1.call-start = ((), (), s32[]{:S(2)}) async-start(), calls=%async_computation.2 | async-start | bytes 917504
  118.9 25.4 %copy-start.2 = (bf16[2,8]{1,0:T(2,128)(2,1)S(1)}, bf16[2,8]{1,0:T(2,128)(2,1)}, u32[]{:S(2)}) copy-start(bf16[2,8]{1,0:T(2,128)(2,1)} %param.14) | copy-start | bytes 100
  118.9 40.2 %copy-start.1 = (bf16[2,7168]{1,0:T(2,128)(2,1)S(1)}, bf16[2,7168]{1,0:T(2,128)(2,1)}, u32[]{:S(2)}) copy-start(bf16[2,7168]{1,0:T(2,128)(2,1)} %param.11) | copy-start | bytes 86020
  140.6 17.9 %all-to-all-start.1 = ((bf16[16,2,7168]{2,1,0:T(2,128)(2,1)}), bf16[16,2,7168]{2,1,0:T(2,128)(2,1)S(1)}, u32[]{:S(2)}, u32[]{:S(2)}) async-start(bf16[16,2,7168]{2,1,0:T(2,128)(2,1)} %reshape.80), calls=%async_computation.1 | async-start | bytes 917504 | tf_op jit(solution)/shard_map/all_to_all | solution.py:74
Sparse Core Ops, SparseCore 0:
  10.7 75.0 all-reduce.2
where the time goes:
time: 168 us
  waiting for transfers between devices  86.8 us (52%)
  matrix products  38.6 us (23%)
  blocking collectives  18.2 us (11%)
  between operations  14.1 us (8%)
  local copies, waits for them, and re-layouts  5.07 us (3%)
  starting transfers between devices  3.56 us (2%)
    unnamed x2, waiting for transfers between devices  72.8 us
    dot_general x1, matrix products, run_expert(): jnp.dot(activated, w_down[0], preferred_element_type=jnp.float32)  20.8 us
    all_to_all x1, blocking collectives, shards(): lax.all_to_all(widened.reshape(expert_count * shard_count, MOST, model_wi...  18.2 us
    all_to_all x1, waiting for transfers between devices, shards(): lax.all_to_all(run_expert(lax.all_to_all(widened.reshape(expert_count * s...  14 us
    dot_general x1, matrix products, run_expert(): gate_val = jnp.dot(flat_rows, w_gate[0], preferred_element_type=jnp.float32)  12 us
    all_to_all x1, starting transfers between devices, shards(): lax.all_to_all(run_expert(lax.all_to_all(widened.reshape(expert_count * s...  3.56 us
  transfers between devices with their start and end apart: 2, of which 2 were waited for; matrix products, arithmetic and copies ran while one was open for 2% of the time, Pallas kernels for 0%

commit v1 on v0

v1 whole, which is shorter than its diff:
```python
import functools

import jax
import jax.numpy as jnp
from jax import lax
from jax.experimental import pallas as pl
from jax.experimental.pallas import tpu as pltpu
from jax.sharding import PartitionSpec as P

GROUP_EXPERTS = 8
MESH = pl.DeviceIdType.MESH


def layer_kernel(
    nodes,
    locals_,
    attn_ref,
    oproj_hbm,
    resid_ref,
    gain_ref,
    routes_ref,
    weight_ref,
    gate_hbm,
    up_hbm,
    down_hbm,
    out_ref,
    oproj,
    slots,
    part_out,
    part_in,
    hidden,
    gathered,
    rows,
    gate_acc,
    up_acc,
    act,
    piece_out,
    piece_in,
    oproj_sem,
    slot_sem,
    part_send,
    part_recv,
    gather_send,
    gather_recv,
    relay_send,
    piece_send,
    piece_recv,
):
    node = lax.axis_index("node")
    local = lax.axis_index("local")
    members = nodes * locals_
    me = node * locals_ + local
    chunk, hidden_units = slots.shape[1], slots.shape[2]
    blocks = hidden_units // chunk
    toks, width = resid_ref.shape
    pairs = width // chunk

    def device(member):
        return {"node": lax.div(member, locals_), "local": lax.rem(member, locals_)}

    def up_copies(i):
        start = pl.ds(pl.multiple_of(i * chunk, chunk), chunk)
        return (
            pltpu.make_async_copy(gate_hbm.at[0, start], slots.at[2 * i], slot_sem.at[2 * i, 0]),
            pltpu.make_async_copy(up_hbm.at[0, start], slots.at[2 * i + 1], slot_sem.at[2 * i + 1, 0]),
        )

    def down_copies(j):
        cols = pl.ds(pl.multiple_of(j * chunk, chunk), chunk)
        return [
            pltpu.make_async_copy(
                down_hbm.at[0, pl.ds(b * chunk, chunk), cols],
                slots.at[j, :, pl.ds(b * chunk, chunk)],
                slot_sem.at[j, b],
            )
            for b in range(blocks)
        ]

    load_oproj = pltpu.make_async_copy(oproj_hbm, oproj, oproj_sem)
    load_oproj.start()

    barrier = pltpu.get_barrier_semaphore()

    def greet(off, carry):
        pl.semaphore_signal(
            barrier, inc=1, device_id=device(lax.rem(me + off, members)), device_id_type=MESH
        )
        return carry

    lax.fori_loop(1, members, greet, 0)

    def fill(i, carry):
        for copy in up_copies(i):
            copy.start()
        return carry

    lax.fori_loop(0, pairs, fill, 0)

    load_oproj.wait()
    for j in range(width // chunk):
        cols = slice(j * chunk, (j + 1) * chunk)
        partial = jnp.dot(attn_ref[...], oproj[:, cols], preferred_element_type=jnp.float32)
        for peer in range(locals_):
            part_out[peer, :, cols] = partial[peer * toks : (peer + 1) * toks].astype(jnp.bfloat16)
    pl.semaphore_wait(barrier, members - 1)

    def part_copy(peer, slot):
        return pltpu.make_async_remote_copy(
            src_ref=part_out.at[peer],
            dst_ref=part_in.at[slot],
            send_sem=part_send.at[peer],
            recv_sem=part_recv.at[slot],
            device_id={"local": peer},
            device_id_type=MESH,
        )

    def send_part(off, carry):
        part_copy(lax.rem(local + off, locals_), local).start()
        return carry

    lax.fori_loop(1, locals_, send_part, 0)
    hidden[...] = resid_ref[...].astype(jnp.float32) + part_out[local].astype(jnp.float32)

    def take_part(off, carry):
        peer = lax.rem(local + off, locals_)
        part_copy(peer, peer).wait_recv()
        hidden[...] += part_in[peer].astype(jnp.float32)
        return carry

    lax.fori_loop(1, locals_, take_part, 0)
    value = hidden[...]
    mean_sq = jnp.mean(value * value, axis=-1, keepdims=True)
    gathered[me] = (value * lax.rsqrt(mean_sq + 1e-06) * gain_ref[...]).astype(jnp.bfloat16)

    def gather_copy(peer, slot):
        return pltpu.make_async_remote_copy(
            src_ref=gathered.at[slot],
            dst_ref=gathered.at[slot],
            send_sem=gather_send.at[peer],
            recv_sem=gather_recv.at[slot],
            device_id={"local": peer},
            device_id_type=MESH,
        )

    def relay_copy(off, slot):
        return pltpu.make_async_remote_copy(
            src_ref=gathered.at[slot],
            dst_ref=gathered.at[slot],
            send_sem=relay_send.at[off, slot],
            recv_sem=gather_recv.at[slot],
            device_id={"node": lax.rem(node + off, nodes)},
            device_id_type=MESH,
        )

    def send_token(off, carry):
        gather_copy(lax.rem(local + off, locals_), me).start()
        return carry

    lax.fori_loop(1, locals_, send_token, 0)
    for off in range(1, nodes):
        relay_copy(off, me).start()

    def take_token(dist, carry):
        peer = lax.rem(local + dist, locals_)
        slot = node * locals_ + peer
        gather_copy(peer, slot).wait_recv()
        for off in range(1, nodes):
            relay_copy(off, slot).start()
        return carry

    lax.fori_loop(1, locals_, take_token, 0)

    def take_relayed(dist, carry):
        peer = lax.rem(local + dist, locals_)
        for off in range(1, nodes):
            relay_copy(off, lax.rem(node + off, nodes) * locals_ + peer).wait_recv()
        return carry

    lax.fori_loop(0, locals_, take_relayed, 0)
    for member in range(members):
        rows[member * toks : (member + 1) * toks, :] = gathered[member]

    gate_acc[...] = jnp.zeros_like(gate_acc)
    up_acc[...] = jnp.zeros_like(up_acc)

    def project_up(i, carry):
        for copy in up_copies(i):
            copy.wait()
        lhs = rows[:, pl.ds(pl.multiple_of(i * chunk, chunk), chunk)]
        gate_acc[...] += jnp.dot(lhs, slots[2 * i], preferred_element_type=jnp.float32)
        up_acc[...] += jnp.dot(lhs, slots[2 * i + 1], preferred_element_type=jnp.float32)
        for late in range(2):
            @pl.when(2 * i + late < pairs)
            def _():
                for copy in down_copies(2 * i + late):
                    copy.start()
        return carry

    lax.fori_loop(0, pairs, project_up, 0)
    gate_val = gate_acc[...]
    act[...] = (gate_val / (1.0 + jnp.exp(-gate_val)) * up_acc[...]).astype(jnp.bfloat16)

    def piece_copy(peer, slot, cols):
        return pltpu.make_async_remote_copy(
            src_ref=piece_out.at[peer, :, cols],
            dst_ref=piece_in.at[slot, :, cols],
            send_sem=piece_send.at[peer],
            recv_sem=piece_recv.at[slot],
            device_id=device(peer),
            device_id_type=MESH,
        )

    def project_down(j, carry):
        for copy in down_copies(j):
            copy.wait()
        cols = pl.ds(pl.multiple_of(j * chunk, chunk), chunk)
        total = jnp.dot(act[:, :chunk], slots[j, :, :chunk], preferred_element_type=jnp.float32)
        for b in range(1, blocks):
            span = slice(b * chunk, (b + 1) * chunk)
            total += jnp.dot(act[:, span], slots[j, :, span], preferred_element_type=jnp.float32)
        for peer in range(members):
            piece_out[peer, :, cols] = total[peer * toks : (peer + 1) * toks].astype(jnp.bfloat16)

        def send_piece(off, inner):
            piece_copy(lax.rem(me + off, members), me, cols).start()
            return inner

        lax.fori_loop(1, members, send_piece, 0)
        return carry

    lax.fori_loop(0, pairs, project_down, 0)
    piece_in[me] = piece_out[me]

    every = pl.ds(0, width)

    def take_piece(off, carry):
        peer = lax.rem(me + off, members)
        piece_copy(peer, peer, every).wait_recv()
        return carry

    shard_count = locals_ // GROUP_EXPERTS
    span = members * toks
    depth = max(8, nodes * toks)
    repeats = depth // toks
    shape = (depth, span)
    row = lax.broadcasted_iota(jnp.int32, shape, 0).astype(jnp.float32)
    col = lax.broadcasted_iota(jnp.int32, shape, 1).astype(jnp.float32)
    row_group = jnp.floor((row + 0.5) * (1.0 / toks))
    row_tok = row - toks * row_group
    col_member = jnp.floor((col + 0.5) * (1.0 / toks))
    col_tok = col - toks * col_member
    col_expert = jnp.floor((col_member + 0.5) * (1.0 / shard_count))
    col_group = jnp.floor((col_expert + 0.5) * (1.0 / GROUP_EXPERTS))
    picks = jnp.concatenate([routes_ref[...].astype(jnp.float32)] * repeats, axis=0)
    scales = jnp.concatenate([weight_ref[...].astype(jnp.float32)] * repeats, axis=0)
    mixing = jnp.zeros(shape, jnp.float32)
    for k in range(picks.shape[1]):
        mixing += jnp.where(picks[:, k : k + 1] == col_expert, scales[:, k : k + 1], 0.0)
    mixing = jnp.where((row_tok == col_tok) & (row_group == col_group), mixing, 0.0).astype(jnp.bfloat16)

    lax.fori_loop(1, members, take_piece, 0)
    for member in range(members):
        rows[member * toks : (member + 1) * toks, :] = piece_in[member]
    for j in range(pairs):
        cols = slice(j * chunk, (j + 1) * chunk)
        mixed = jnp.dot(mixing, rows[:, cols], preferred_element_type=jnp.float32)
        summed = hidden[:, cols]
        for group in range(nodes):
            group_out = mixed[group * toks : (group + 1) * toks].astype(jnp.bfloat16)
            summed = summed + group_out.astype(jnp.float32)
        out_ref[:, cols] = summed.astype(jnp.bfloat16)

    def drain_local(off, carry):
        peer = lax.rem(local + off, locals_)
        part_copy(peer, local).wait_send()
        gather_copy(peer, me).wait_send()
        return carry

    lax.fori_loop(1, locals_, drain_local, 0)

    def drain_relay(peer, carry):
        for off in range(1, nodes):
            relay_copy(off, node * locals_ + peer).wait_send()
        return carry

    lax.fori_loop(0, locals_, drain_relay, 0)

    def drain_piece(off, carry):
        piece_copy(lax.rem(me + off, members), me, every).wait_send()
        return carry

    lax.fori_loop(1, members, drain_piece, 0)


def solution(mesh):
    nodes, locals_ = mesh.shape["node"], mesh.shape["local"]
    members = nodes * locals_

    def shards(attn_out, o_proj, resid, norm_gain, routes, route_w, w_gate, w_up, w_down):
        toks, width = resid.shape
        hidden_units = w_gate.shape[2]
        chunk = next(c for c in (512, 256, 128) if hidden_units % c == 0 and width % c == 0)
        pairs = width // chunk
        blocks = hidden_units // chunk
        bf16, f32 = jnp.bfloat16, jnp.float32
        vmem = pl.BlockSpec(memory_space=pltpu.VMEM)
        hbm = pl.BlockSpec(memory_space=pl.ANY)
        dma = pltpu.SemaphoreType.DMA
        total = members * toks
        return pl.pallas_call(
            functools.partial(layer_kernel, nodes, locals_),
            out_shape=jax.ShapeDtypeStruct((toks, width), bf16),
            in_specs=[vmem, hbm, vmem, vmem, vmem, vmem, hbm, hbm, hbm],
            out_specs=vmem,
            scratch_shapes=[
                pltpu.VMEM(o_proj.shape, bf16),
                pltpu.VMEM((2 * pairs, chunk, hidden_units), bf16),
                pltpu.VMEM((locals_, toks, width), bf16),
                pltpu.VMEM((locals_, toks, width), bf16),
                pltpu.VMEM((toks, width), f32),
                pltpu.VMEM((members, toks, width), bf16),
                pltpu.VMEM((total, width), bf16),
                pltpu.VMEM((total, hidden_units), f32),
                pltpu.VMEM((total, hidden_units), f32),
                pltpu.VMEM((total, hidden_units), bf16),
                pltpu.VMEM((members, toks, width), bf16),
                pltpu.VMEM((members, toks, width), bf16),
                dma,
                dma((2 * pairs, blocks)),
                dma((locals_,)),
                dma((locals_,)),
                dma((locals_,)),
                dma((members,)),
                dma((nodes, members)),
                dma((members,)),
                dma((members,)),
            ],
            compiler_params=pltpu.CompilerParams(
                collective_id=0, has_side_effects=True, vmem_limit_bytes=67043328
            ),
            name="moe_layer",
        )(attn_out, o_proj, resid, norm_gain.reshape(1, width), routes, route_w, w_gate, w_up, w_down)

    placed = (
        P(("rep", "node"), "local"),
        P("local", None),
        P(("rep", "node", "local"), None),
        P(),
        P(("rep", "node", "local"), None),
        P(("rep", "node", "local"), None),
        P(("node", "local"), None, None),
        P(("node", "local"), None, None),
        P(("node", "local"), None, None),
    )
    return jax.shard_map(
        shards,
        mesh=mesh,
        in_specs=placed,
        out_specs=P(("rep", "node", "local"), None),
        check_vma=False,
    )
```

time: 168 us -> 52.2 us (0.31)
  waiting for transfers between devices: 86.8 us -> 0 us
  Pallas kernels: 0 us -> 50.6 us
  matrix products: 38.6 us -> 0 us
  blocking collectives: 18.2 us -> 0 us
  between operations: 14.1 us -> 0.01 us
  local copies, waits for them, and re-layouts: 5.07 us -> 1.38 us
  starting transfers between devices: 3.56 us -> 0 us
    unnamed x2 -> x0, waiting for transfers between devices: 72.8 us -> none
    pallas_call x0 -> x1, Pallas kernels: none -> 50.6 us  [shards(): pl.pallas_call(functools.partial(layer_kernel, nodes, locals_), out_shape...]
    dot_general x8 -> x0, matrix products: 38.6 us -> none  [the longest x1 20.8 us: run_expert(): jnp.dot(activated, w_down[0], preferred_element_type=jnp.float32)]
    all_to_all x1 -> x0, blocking collectives: 18.2 us -> none  [shards(): lax.all_to_all(widened.reshape(expert_count * shard_count, MOST, model_wi...]
    all_to_all x1 -> x0, waiting for transfers between devices: 14 us -> none  [shards(): lax.all_to_all(run_expert(lax.all_to_all(widened.reshape(expert_count * s...]
    all_to_all x1 -> x0, starting transfers between devices: 3.56 us -> none  [shards(): lax.all_to_all(run_expert(lax.all_to_all(widened.reshape(expert_count * s...]
    reshape x4 -> x0, local copies, waits for them, and re-layouts: 2.06 us -> none  [the longest x1 0.96 us: run_expert(): return pieces.reshape(senders, slot_count, model_width)]
  transfers between devices with their start and end apart: 2 -> 0, of which waited for: 2 -> 0; matrix products, arithmetic and copies ran while one was open for 2% -> 0% of each run, Pallas kernels for 0% -> 0%
where the time goes in v1:
time: 52.2 us; the launch traced here: 52 us
  Pallas kernels  50.6 us (97%)
  local copies, waits for them, and re-layouts  1.38 us (3%)
    pallas_call x1, Pallas kernels, shards(): pl.pallas_call(functools.partial(layer_kernel, nodes, locals_), out_shape...  50.6 us
    unnamed x1, local copies, waits for them, and re-layouts  1.38 us

profile of v1, /device:TPU:0, one launch (start us, length us, event | category | flops | bytes accessed | tf_op | source)
XLA Modules:
  0.0 52.0 jit_solution(1970479909339979794)
XLA Ops:
  0.0 50.6 %moe_layer.1 = bf16[2,7168]{1,0:T(2,128)(2,1)} custom-call(bf16[16,128]{1,0:T(8,128)(2,1)} %attn_ref.1, bf16[128,7168]{1,0:T(8,128)(2,1)} %oproj_hbm.1, bf16[2,7168]{1,0:T(2,128)(2,1)} %resid_ref.1, f32[1,7168]{1,0:T(1,128)} %bitcast.1, s32[2,8]{1,0:T(2,128)} %routes_ref.1, bf16[2,8]{1,0:T(2,128)(2,1)} %weight_ref.1, bf16[1,7168,2048]{2,1,0:T(8,128)(2,1)} %gate_hbm.1, ...), custom_call_target="tpu_custom_call" | custom-call | tf_op jit(solution)/shard_map/moe_layer/pallas_call | solution.py:310
  50.6 1.4 %copy.11 = bf16[2,7168]{1,0:T(2,128)(2,1)} copy(bf16[2,7168]{1,0:T(2,128)(2,1)} %moe_layer.1) | data formatting | bytes 57344

commit v2 on v1

v2 whole, which is shorter than its diff:
```python
import functools

import jax
import jax.numpy as jnp
from jax import lax
from jax.experimental import pallas as pl
from jax.experimental.pallas import tpu as pltpu
from jax.sharding import PartitionSpec as P

GROUP_EXPERTS = 8
MESH = pl.DeviceIdType.MESH


def layer_kernel(
    nodes,
    locals_,
    stages,
    attn_ref,
    oproj_hbm,
    resid_ref,
    gain_ref,
    routes_ref,
    weight_ref,
    gate_hbm,
    up_hbm,
    down_hbm,
    out_ref,
    oproj,
    slots,
    part_out,
    part_in,
    hidden,
    gathered,
    rows,
    meta,
    meta_rows,
    gate_acc,
    up_acc,
    act,
    weighted,
    cross_out,
    cross_in,
    piece_out,
    piece_in,
    oproj_sem,
    slot_sem,
    part_send,
    part_recv,
    gather_send,
    gather_recv,
    relay_send,
    meta_send,
    meta_recv,
    meta_relay_send,
    cross_send,
    cross_recv,
    piece_send,
    piece_recv,
):
    node = lax.axis_index("node")
    local = lax.axis_index("local")
    members = nodes * locals_
    me = node * locals_ + local
    chunk, hidden_units = slots.shape[1], slots.shape[2]
    blocks = hidden_units // chunk
    toks, width = resid_ref.shape
    pairs = width // chunk
    stage_width = width // stages
    stage_pairs = pairs // stages
    half = locals_ * toks
    every = pl.ds(0, width)

    def stage_cols(s):
        return every if s is None else pl.ds(s * stage_width, stage_width)

    def chunk_cols(j):
        return pl.ds(pl.multiple_of(j * chunk, chunk), chunk)

    def peer_loop(first, body):
        def step(dist, carry):
            body(lax.rem(local + dist, locals_))
            return carry

        lax.fori_loop(first, locals_, step, 0)

    def up_copies(i):
        return (
            pltpu.make_async_copy(gate_hbm.at[0, chunk_cols(i)], slots.at[2 * i], slot_sem.at[2 * i, 0]),
            pltpu.make_async_copy(up_hbm.at[0, chunk_cols(i)], slots.at[2 * i + 1], slot_sem.at[2 * i + 1, 0]),
        )

    def down_copies(j):
        return [
            pltpu.make_async_copy(
                down_hbm.at[0, pl.ds(b * chunk, chunk), chunk_cols(j)],
                slots.at[j, :, pl.ds(b * chunk, chunk)],
                slot_sem.at[j, b],
            )
            for b in range(blocks)
        ]

    load_oproj = pltpu.make_async_copy(oproj_hbm, oproj, oproj_sem)
    load_oproj.start()

    barrier = pltpu.get_barrier_semaphore()

    def greet(peer):
        pl.semaphore_signal(barrier, inc=1, device_id={"local": peer}, device_id_type=MESH)

    peer_loop(1, greet)
    for off in range(1, nodes):
        pl.semaphore_signal(
            barrier, inc=1, device_id={"node": lax.rem(node + off, nodes)}, device_id_type=MESH
        )

    def fill(i, carry):
        for copy in up_copies(i):
            copy.start()
        return carry

    lax.fori_loop(0, pairs, fill, 0)

    def part_copy(peer, slot, s):
        return pltpu.make_async_remote_copy(
            src_ref=part_out.at[peer, :, stage_cols(s)],
            dst_ref=part_in.at[slot, :, stage_cols(s)],
            send_sem=part_send.at[peer],
            recv_sem=part_recv.at[slot, s or 0],
            device_id={"local": peer},
            device_id_type=MESH,
        )

    def gather_copy(peer, slot, s):
        return pltpu.make_async_remote_copy(
            src_ref=gathered.at[slot, :, stage_cols(s)],
            dst_ref=gathered.at[slot, :, stage_cols(s)],
            send_sem=gather_send.at[peer],
            recv_sem=gather_recv.at[slot, s or 0],
            device_id={"local": peer},
            device_id_type=MESH,
        )

    def relay_copy(off, slot, s):
        return pltpu.make_async_remote_copy(
            src_ref=gathered.at[slot, :, stage_cols(s)],
            dst_ref=gathered.at[slot, :, stage_cols(s)],
            send_sem=relay_send.at[off - 1, lax.rem(slot, locals_)],
            recv_sem=gather_recv.at[slot, s or 0],
            device_id={"node": lax.rem(node + off, nodes)},
            device_id_type=MESH,
        )

    def meta_copy(peer, slot):
        return pltpu.make_async_remote_copy(
            src_ref=meta.at[slot],
            dst_ref=meta.at[slot],
            send_sem=meta_send.at[peer],
            recv_sem=meta_recv.at[slot],
            device_id={"local": peer},
            device_id_type=MESH,
        )

    def meta_relay(off, slot):
        return pltpu.make_async_remote_copy(
            src_ref=meta.at[slot],
            dst_ref=meta.at[slot],
            send_sem=meta_relay_send.at[off - 1, lax.rem(slot, locals_)],
            recv_sem=meta_recv.at[slot],
            device_id={"node": lax.rem(node + off, nodes)},
            device_id_type=MESH,
        )

    load_oproj.wait()
    for s in range(stages):
        cols = stage_cols(s)
        partial = jnp.dot(attn_ref[...], oproj[:, cols], preferred_element_type=jnp.float32)
        for peer in range(locals_):
            part_out[peer, :, cols] = partial[peer * toks : (peer + 1) * toks].astype(jnp.bfloat16)
        if s == 0:
            pl.semaphore_wait(barrier, locals_ - 1 + nodes - 1)
        peer_loop(1, lambda peer: part_copy(peer, local, s).start())

    gate_acc[...] = jnp.zeros_like(gate_acc)
    up_acc[...] = jnp.zeros_like(up_acc)

    def reduce_stage(s):
        cols = stage_cols(s)
        peer_loop(1, lambda peer: part_copy(peer, peer, s).wait_recv())
        part_in[local, :, cols] = part_out[local, :, cols]
        value = resid_ref[:, cols].astype(jnp.float32)
        for peer in range(locals_):
            value += part_in[peer, :, cols].astype(jnp.float32)
        hidden[:, cols] = value
        gathered[me, :, cols] = (value * gain_ref[:, cols]).astype(jnp.bfloat16)
        peer_loop(1, lambda peer: gather_copy(peer, me, s).start())
        for off in range(1, nodes):
            relay_copy(off, me, s).start()

    def send_meta():
        value = hidden[...]
        scale = lax.rsqrt(jnp.mean(value * value, axis=-1, keepdims=True) + 1e-06)
        lane = lax.broadcasted_iota(jnp.int32, (toks, 128), 1)
        picks, scales = routes_ref[...], weight_ref[...].astype(jnp.float32)
        shares = jnp.zeros((toks, 128), jnp.float32)
        for k in range(picks.shape[1]):
            shares += jnp.where(picks[:, k : k + 1] == lane, scales[:, k : k + 1], 0.0)
        meta[me] = jnp.where(lane == 127, scale, shares)
        peer_loop(1, lambda peer: meta_copy(peer, me).start())
        for off in range(1, nodes):
            meta_relay(off, me).start()

    def relay_stage(s):
        def forward(peer):
            slot = node * locals_ + peer
            gather_copy(peer, slot, s).wait_recv()
            for off in range(1, nodes):
                relay_copy(off, slot, s).start()

        peer_loop(1, forward)

    def project_up(i, carry):
        for copy in up_copies(i):
            copy.wait()
        lhs = rows[:, chunk_cols(i)]
        gate_acc[...] += jnp.dot(lhs, slots[2 * i], preferred_element_type=jnp.float32)
        up_acc[...] += jnp.dot(lhs, slots[2 * i + 1], preferred_element_type=jnp.float32)
        for late in range(2):

            @pl.when(2 * i + late < pairs)
            def _():
                for copy in down_copies(2 * i + late):
                    copy.start()

        return carry

    def multiply_stage(s):
        def arrive(peer):
            for off in range(1, nodes):
                relay_copy(off, lax.rem(node + off, nodes) * locals_ + peer, s).wait_recv()

        peer_loop(0, arrive)
        cols = stage_cols(s)
        for member in range(members):
            rows[member * toks : (member + 1) * toks, cols] = gathered[member, :, cols]
        lax.fori_loop(s * stage_pairs, (s + 1) * stage_pairs, project_up, 0)

    for step in range(stages + 2):
        if step < stages:
            reduce_stage(step)
        if step == stages - 1:
            send_meta()
        if 1 <= step <= stages:
            relay_stage(step - 1)
        if step == stages:

            def forward_meta(peer):
                slot = node * locals_ + peer
                meta_copy(peer, slot).wait_recv()
                for off in range(1, nodes):
                    meta_relay(off, slot).start()

            peer_loop(1, forward_meta)
        if step >= 2:
            multiply_stage(step - 2)

    def meta_arrive(peer):
        for off in range(1, nodes):
            meta_relay(off, lax.rem(node + off, nodes) * locals_ + peer).wait_recv()

    peer_loop(0, meta_arrive)
    for member in range(members):
        meta_rows[member * toks : (member + 1) * toks, :] = meta[member]
    facts = meta_rows[...]
    lane = lax.broadcasted_iota(jnp.int32, facts.shape, 1)
    expert = lax.div(me, locals_ // GROUP_EXPERTS)
    share = jnp.sum(jnp.where(lane == expert, facts, 0.0), axis=1, keepdims=True)
    scale = jnp.sum(jnp.where(lane == 127, facts, 0.0), axis=1, keepdims=True)
    for b in range(blocks):
        span = slice(b * chunk, (b + 1) * chunk)
        gate_val = gate_acc[:, span] * scale
        up_val = up_acc[:, span] * (scale * share)
        act[:, span] = (gate_val / (1.0 + jnp.exp(-gate_val)) * up_val).astype(jnp.bfloat16)

    def cross_copy(off, j):
        return pltpu.make_async_remote_copy(
            src_ref=cross_out.at[off - 1, j],
            dst_ref=cross_in.at[off - 1, j],
            send_sem=cross_send.at[off - 1, j],
            recv_sem=cross_recv.at[off - 1, j],
            device_id={"node": lax.rem(node + off, nodes)},
            device_id_type=MESH,
        )

    def piece_copy(peer, slot, cols):
        return pltpu.make_async_remote_copy(
            src_ref=piece_out.at[peer, :, cols],
            dst_ref=piece_in.at[slot, :, cols],
            send_sem=piece_send.at[peer],
            recv_sem=piece_recv.at[slot],
            device_id={"local": peer},
            device_id_type=MESH,
        )

    def project_down(j):
        for copy in down_copies(j):
            copy.wait()
        total = jnp.dot(act[:, :chunk], slots[j, :, :chunk], preferred_element_type=jnp.float32)
        for b in range(1, blocks):
            span = slice(b * chunk, (b + 1) * chunk)
            total += jnp.dot(act[:, span], slots[j, :, span], preferred_element_type=jnp.float32)
        for group in range(nodes):
            weighted[j, group] = total[group * half : (group + 1) * half]
        for off in range(1, nodes):
            cross_out[off - 1, j] = weighted[j, lax.rem(node + off, nodes)].astype(jnp.bfloat16)
            cross_copy(off, j).start()

    def send_pieces(j):
        total = weighted[j, node]
        for off in range(1, nodes):
            cross_copy(off, j).wait_recv()
            total += cross_in[off - 1, j].astype(jnp.float32)
        cols = chunk_cols(j)
        for peer in range(locals_):
            piece_out[peer, :, cols] = total[peer * toks : (peer + 1) * toks].astype(jnp.bfloat16)
        peer_loop(1, lambda peer: piece_copy(peer, local, cols).start())

    project_down(0)

    def down_step(j, carry):
        project_down(j)
        send_pieces(j - 1)
        return carry

    lax.fori_loop(1, pairs, down_step, 0)
    send_pieces(pairs - 1)
    piece_in[local] = piece_out[local]
    peer_loop(1, lambda peer: piece_copy(peer, peer, every).wait_recv())
    for s in range(stages):
        cols = stage_cols(s)
        summed = hidden[:, cols]
        for peer in range(locals_):
            summed += piece_in[peer, :, cols].astype(jnp.float32)
        out_ref[:, cols] = summed.astype(jnp.bfloat16)

    def drain(peer):
        part_copy(peer, local, None).wait_send()
        gather_copy(peer, me, None).wait_send()
        meta_copy(peer, me).wait_send()
        piece_copy(peer, local, every).wait_send()

    peer_loop(1, drain)

    def drain_relay(peer):
        for off in range(1, nodes):
            relay_copy(off, node * locals_ + peer, None).wait_send()
            meta_relay(off, node * locals_ + peer).wait_send()

    peer_loop(0, drain_relay)

    def drain_cross(j, carry):
        for off in range(1, nodes):
            cross_copy(off, j).wait_send()
        return carry

    lax.fori_loop(0, pairs, drain_cross, 0)


def solution(mesh):
    nodes, locals_ = mesh.shape["node"], mesh.shape["local"]
    members = nodes * locals_

    def shards(attn_out, o_proj, resid, norm_gain, routes, route_w, w_gate, w_up, w_down):
        toks, width = resid.shape
        hidden_units = w_gate.shape[2]
        chunk = next(c for c in (512, 256, 128) if hidden_units % c == 0 and width % c == 0)
        pairs = width // chunk
        blocks = hidden_units // chunk
        stages = next(n for n in (7, 4, 2, 1) if pairs % n == 0)
        bf16, f32 = jnp.bfloat16, jnp.float32
        vmem = pl.BlockSpec(memory_space=pltpu.VMEM)
        hbm = pl.BlockSpec(memory_space=pl.ANY)
        dma = pltpu.SemaphoreType.DMA
        total = members * toks
        return pl.pallas_call(
            functools.partial(layer_kernel, nodes, locals_, stages),
            out_shape=jax.ShapeDtypeStruct((toks, width), bf16),
            in_specs=[vmem, hbm, vmem, vmem, vmem, vmem, hbm, hbm, hbm],
            out_specs=vmem,
            scratch_shapes=[
                pltpu.VMEM(o_proj.shape, bf16),
                pltpu.VMEM((2 * pairs, chunk, hidden_units), bf16),
                pltpu.VMEM((locals_, toks, width), bf16),
                pltpu.VMEM((locals_, toks, width), bf16),
                pltpu.VMEM((toks, width), f32),
                pltpu.VMEM((members, toks, width), bf16),
                pltpu.VMEM((total, width), bf16),
                pltpu.VMEM((members, toks, 128), f32),
                pltpu.VMEM((total, 128), f32),
                pltpu.VMEM((total, hidden_units), f32),
                pltpu.VMEM((total, hidden_units), f32),
                pltpu.VMEM((total, hidden_units), bf16),
                pltpu.VMEM((pairs, nodes, locals_ * toks, chunk), f32),
                pltpu.VMEM((nodes - 1, pairs, locals_ * toks, chunk), bf16),
                pltpu.VMEM((nodes - 1, pairs, locals_ * toks, chunk), bf16),
                pltpu.VMEM((locals_, toks, width), bf16),
                pltpu.VMEM((locals_, toks, width), bf16),
                dma,
                dma((2 * pairs, blocks)),
                dma((locals_,)),
                dma((locals_, stages)),
                dma((locals_,)),
                dma((members, stages)),
                dma((nodes - 1, locals_)),
                dma((locals_,)),
                dma((members,)),
                dma((nodes - 1, locals_)),
                dma((nodes - 1, pairs)),
                dma((nodes - 1, pairs)),
                dma((locals_,)),
                dma((locals_,)),
            ],
            compiler_params=pltpu.CompilerParams(
                collective_id=0, has_side_effects=True, vmem_limit_bytes=67043328
            ),
            name="moe_layer",
        )(attn_out, o_proj, resid, norm_gain.reshape(1, width), routes, route_w, w_gate, w_up, w_down)

    placed = (
        P(("rep", "node"), "local"),
        P("local", None),
        P(("rep", "node", "local"), None),
        P(),
        P(("rep", "node", "local"), None),
        P(("rep", "node", "local"), None),
        P(("node", "local"), None, None),
        P(("node", "local"), None, None),
        P(("node", "local"), None, None),
    )
    return jax.shard_map(
        shards,
        mesh=mesh,
        in_specs=placed,
        out_specs=P(("rep", "node", "local"), None),
        check_vma=False,
    )
```

time: 52.2 us -> 55.7 us (1.067)
  Pallas kernels: 50.6 us -> 54.1 us
    pallas_call x1, Pallas kernels: 50.6 us -> 54.1 us  [shards(): pl.pallas_call(functools.partial(layer_kernel, nodes, locals_, stages), o...]
where the time goes in v2:
time: 55.7 us; the launch traced here: 55.5 us
  Pallas kernels  54.1 us (97%)
  local copies, waits for them, and re-layouts  1.38 us (2%)
    pallas_call x1, Pallas kernels, shards(): pl.pallas_call(functools.partial(layer_kernel, nodes, locals_, stages), o...  54.1 us
    unnamed x1, local copies, waits for them, and re-layouts  1.38 us

profile of v2, /device:TPU:0, one launch (start us, length us, event | category | flops | bytes accessed | tf_op | source)
XLA Modules:
  0.0 55.5 jit_solution(2132880632315632465)
XLA Ops:
  0.0 54.1 %moe_layer.1 = bf16[2,7168]{1,0:T(2,128)(2,1)} custom-call(bf16[16,128]{1,0:T(8,128)(2,1)} %attn_ref.1, bf16[128,7168]{1,0:T(8,128)(2,1)} %oproj_hbm.1, bf16[2,7168]{1,0:T(2,128)(2,1)} %resid_ref.1, f32[1,7168]{1,0:T(1,128)} %bitcast.1, s32[2,8]{1,0:T(2,128)} %routes_ref.1, bf16[2,8]{1,0:T(2,128)(2,1)} %weight_ref.1, bf16[1,7168,2048]{2,1,0:T(8,128)(2,1)} %gate_hbm.1, ...), custom_call_target="tpu_custom_call" | custom-call | tf_op jit(solution)/shard_map/moe_layer/pallas_call | solution.py:384
  54.1 1.4 %copy.11 = bf16[2,7168]{1,0:T(2,128)(2,1)} copy(bf16[2,7168]{1,0:T(2,128)(2,1)} %moe_layer.1) | data formatting | bytes 57344

commit v3 on v2

--- a/solution.py
+++ b/solution.py
@@ -68,6 +68,8 @@
     stage_width = width // stages
     stage_pairs = pairs // stages
     half = locals_ * toks
+    group_chunks = 2 if pairs % 2 == 0 else 1
+    lag = min(3, pairs)
     every = pl.ds(0, width)
 
     def stage_cols(s):
@@ -322,17 +324,29 @@
         cols = chunk_cols(j)
         for peer in range(locals_):
             piece_out[peer, :, cols] = total[peer * toks : (peer + 1) * toks].astype(jnp.bfloat16)
-        peer_loop(1, lambda peer: piece_copy(peer, local, cols).start())
-
-    project_down(0)
+
+        @pl.when(j % group_chunks == group_chunks - 1)
+        def _():
+            first = pl.multiple_of((j - group_chunks + 1) * chunk, chunk)
+            sent = pl.ds(first, group_chunks * chunk)
+            peer_loop(1, lambda peer: piece_copy(peer, local, sent).start())
+
+    def down_start(j, carry):
+        project_down(j)
+        return carry
 
     def down_step(j, carry):
         project_down(j)
-        send_pieces(j - 1)
-        return carry
-
-    lax.fori_loop(1, pairs, down_step, 0)
-    send_pieces(pairs - 1)
+        send_pieces(j - lag)
+        return carry
+
+    def down_finish(j, carry):
+        send_pieces(j)
+        return carry
+
+    lax.fori_loop(0, lag, down_start, 0)
+    lax.fori_loop(lag, pairs, down_step, 0)
+    lax.fori_loop(pairs - lag, pairs, down_finish, 0)
     piece_in[local] = piece_out[local]
     peer_loop(1, lambda peer: piece_copy(peer, peer, every).wait_recv())
     for s in range(stages):
@@ -375,7 +389,7 @@
         chunk = next(c for c in (512, 256, 128) if hidden_units % c == 0 and width % c == 0)
         pairs = width // chunk
         blocks = hidden_units // chunk
-        stages = next(n for n in (7, 4, 2, 1) if pairs % n == 0)
+        stages = next(n for n in (2, 1) if pairs % n == 0)
         bf16, f32 = jnp.bfloat16, jnp.float32
         vmem = pl.BlockSpec(memory_space=pltpu.VMEM)
         hbm = pl.BlockSpec(memory_space=pl.ANY)

time: 55.7 us -> 48.4 us (0.87)
  Pallas kernels: 54.1 us -> 46.8 us
    pallas_call x1, Pallas kernels: 54.1 us -> 46.8 us  [shards(): pl.pallas_call(functools.partial(layer_kernel, nodes, locals_, stages), o...]
where the time goes in v3:
time: 48.4 us; the launch traced here: 48.2 us
  Pallas kernels  46.8 us (97%)
  local copies, waits for them, and re-layouts  1.38 us (3%)
    pallas_call x1, Pallas kernels, shards(): pl.pallas_call(functools.partial(layer_kernel, nodes, locals_, stages), o...  46.8 us
    unnamed x1, local copies, waits for them, and re-layouts  1.38 us

profile of v3, /device:TPU:0, one launch (start us, length us, event | category | flops | bytes accessed | tf_op | source)
XLA Modules:
  0.0 48.2 jit_solution(10213067565505370857)
XLA Ops:
  0.0 46.8 %moe_layer.1 = bf16[2,7168]{1,0:T(2,128)(2,1)} custom-call(bf16[16,128]{1,0:T(8,128)(2,1)} %attn_ref.1, bf16[128,7168]{1,0:T(8,128)(2,1)} %oproj_hbm.1, bf16[2,7168]{1,0:T(2,128)(2,1)} %resid_ref.1, f32[1,7168]{1,0:T(1,128)} %bitcast.1, s32[2,8]{1,0:T(2,128)} %routes_ref.1, bf16[2,8]{1,0:T(2,128)(2,1)} %weight_ref.1, bf16[1,7168,2048]{2,1,0:T(8,128)(2,1)} %gate_hbm.1, ...), custom_call_target="tpu_custom_call" | custom-call | tf_op jit(solution)/shard_map/moe_layer/pallas_call | solution.py:398
  46.8 1.4 %copy.11 = bf16[2,7168]{1,0:T(2,128)(2,1)} copy(bf16[2,7168]{1,0:T(2,128)(2,1)} %moe_layer.1) | data formatting | bytes 57344
